TPU v7x, 32 devices: a whole 2x2x4 slice. The times are simulated.
32 devices in a mesh: aa: 4 (over z), ba: 8 (over y, x, core).
Axes of the slice: x: 2, y: 2, z: 4, core: 2. Of those that a mesh axis runs over, the one named last changes fastest.
Arguments:
- feats: bfloat16 [4, 32, 128, 256], P('aa', 'ba'), may hold values from -6 to 6
- conv_one: bfloat16 [3, 3, 3, 256, 256], replicated, may hold values from -0.078125 to 0.078125
- bias_one: float32 [256], replicated, may hold values from -3 to 3
- conv_two: bfloat16 [3, 3, 3, 256, 256], replicated, may hold values from -0.078125 to 0.078125
- bias_two: float32 [256], replicated, may hold values from -3 to 3
- patch_weight: bfloat16 [2, 2, 256, 128], replicated, may hold values from -0.1875 to 0.1875
- patch_bias: float32 [128], replicated, may hold values from -3 to 3
- embed_weight: bfloat16 [128, 2048], replicated, may hold values from -0.5 to 0.5
- embed_bias: float32 [2048], replicated, may hold values from -6 to 6
- norm_gain: float32 [2048], replicated, may hold values from 0.1 to 1.9
- w_query: bfloat16 [2048, 2048], P(None, 'ba'), may hold values from -2 to 2
- w_key: bfloat16 [2048, 2048], P(None, 'ba'), may hold values from -2 to 2
- w_value: bfloat16 [2048, 2048], P(None, 'ba'), may hold values from -0.125 to 0.125
- w_velocity: bfloat16 [2048, 128], P('ba'), may hold values from -0.5 to 0.5
Outputs:
- velocity: float32 [4096, 128], P(('aa', 'ba'))
All inputs are finite; a program needn't handle non-finite values.
Results may differ from a plain program's by a relative error of at most 0.035.
Values may be sent and summed in bfloat16 or wider, within the bound.
A program may use at most 128 MiB of HBM per device.

v0:
```python
import functools
import math

import jax
import jax.numpy as jnp
from jax import lax
from jax.experimental import pallas as pl
from jax.experimental.pallas import tpu as pltpu
from jax.sharding import PartitionSpec as P

HEAD_DIM = 64
SLOT = 128
MESH = pl.DeviceIdType.MESH
F32 = jnp.float32
BF16 = jnp.bfloat16
VMEM_BYTES = 67043328


def dot(left, right):
    return jnp.dot(left, right, preferred_element_type=F32)


def two_parts(value):
    high = value.astype(BF16)
    return high, (value - high.astype(F32)).astype(BF16)


def gelu(value):
    return 0.5 * value * (1.0 + lax.erf(value * (0.5**0.5)))


def whole_kernel(
    n_aa, n_ba, span, chunk,
    feats, conv_one, bias_one, conv_two, bias_two, patch_weight, patch_bias,
    embed_weight, embed_bias, norm_gain, w_query, w_key, w_value, w_velocity,
    out,
    field_one, field_two, taps, w_joined, acc, pair, gathered, split, offsets, gram_split, gram,
    queries, keys, values, shares, arrived,
    load_sem, aa_side_send, aa_side_recv, ba_side_send, ba_side_recv,
    aa_send, aa_recv, ba_send, ba_recv, core_send, core_recv, share_send, share_recv,
):
    aa, ba = lax.axis_index("aa"), lax.axis_index("ba")
    _, rows, width, chans = feats.shape
    partner = ba + 1 - 2 * (ba % 2)
    half = n_ba // 2
    heads = w_query.shape[1] // HEAD_DIM
    tokens = rows * width // 4
    lat = patch_bias.shape[1]

    def load(source, target, at):
        return pltpu.make_async_copy(source, target, load_sem.at[at])

    loads = [
        load(feats.at[0], field_one.at[1, pl.ds(1, rows)], 0),
        load(conv_one, taps, 1),
        load(w_query, w_joined.at[0], 2),
        load(w_key, w_joined.at[1], 3),
        load(w_value, w_joined.at[2], 4),
    ]
    for one in loads:
        one.start()

    def aa_there(side):
        return aa > 0 if side == -1 else aa < n_aa - 1

    def ba_there(side):
        return ba > 0 if side == -1 else ba < n_ba - 1

    barrier = pltpu.get_barrier_semaphore()
    for step in range(1, n_aa):
        pl.semaphore_signal(
            barrier, inc=1, device_id=((aa + step) % n_aa, ba), device_id_type=MESH
        )
    for step in range(1, n_ba):
        pl.semaphore_signal(
            barrier, inc=1, device_id=(aa, (ba + step) % n_ba), device_id_type=MESH
        )

    def along_time(field, side, piece):
        row = (slice(1, 2), slice(rows, rows + 1), slice(2, rows))[piece]
        at = (0 if field is field_one else 1, (side + 1) // 2, piece)
        return pltpu.make_async_remote_copy(
            src_ref=field.at[1, row], dst_ref=field.at[1 - side, row],
            send_sem=aa_side_send.at[at], recv_sem=aa_side_recv.at[at],
            device_id=(aa + side, ba), device_id_type=MESH,
        )

    def along_rows(field, frame, side):
        source, target = (rows, 0) if side == 1 else (1, rows + 1)
        at = (0 if field is field_one else 1, frame, (side + 1) // 2)
        return pltpu.make_async_remote_copy(
            src_ref=field.at[frame, pl.ds(source, 1)], dst_ref=field.at[frame, pl.ds(target, 1)],
            send_sem=ba_side_send.at[at], recv_sem=ba_side_recv.at[at],
            device_id=(aa, ba + side), device_id_type=MESH,
        )

    def send_field(field):
        for side in (-1, 1):
            pl.when(ba_there(side))(along_rows(field, 1, side).start)
        for piece in range(3):
            for side in (-1, 1):
                pl.when(aa_there(side))(along_time(field, side, piece).start)

    def take_time(field, pieces):
        for side in (-1, 1):
            @pl.when(aa_there(-side))
            def _():
                for piece in pieces:
                    along_time(field, side, piece).wait_recv()

    def relay_rows(field):
        for frame, behind in ((0, -1), (2, 1)):
            for side in (-1, 1):
                pl.when(jnp.logical_and(aa_there(behind), ba_there(side)))(
                    along_rows(field, frame, side).start
                )

    def take_rows(field, frame):
        for side in (-1, 1):
            inside = ba_there(-side)
            if frame != 1:
                inside = jnp.logical_and(inside, aa_there(frame - 1))
            pl.when(inside)(along_rows(field, frame, side).wait_recv)

    def sent(field):
        for side in (-1, 1):
            @pl.when(aa_there(side))
            def _():
                for piece in range(3):
                    along_time(field, side, piece).wait_send()

            pl.when(ba_there(side))(along_rows(field, 1, side).wait_send)
            for frame, behind in ((0, -1), (2, 1)):
                pl.when(jnp.logical_and(aa_there(behind), ba_there(side)))(
                    along_rows(field, frame, side).wait_send
                )

    def blank(field):
        line = jnp.zeros((width, chans), BF16)
        for frame, behind in ((0, -1), (2, 1)):
            @pl.when(jnp.logical_not(aa_there(behind)))
            def _():
                for row in range(rows + 2):
                    field[frame, row] = line

            @pl.when(aa_there(behind))
            def _():
                for side, row in ((-1, 0), (1, rows + 1)):
                    @pl.when(jnp.logical_not(ba_there(side)))
                    def _():
                        field[frame, row] = line
        for side, row in ((-1, 0), (1, rows + 1)):
            @pl.when(jnp.logical_not(ba_there(side)))
            def _():
                field[1, row] = line

    blank(field_one)
    blank(field_two)
    pl.semaphore_wait(barrier, n_aa - 1 + n_ba - 1)
    loads[0].wait()
    send_field(field_one)

    def merge_weights():
        embed = embed_weight[...].astype(F32)
        centred = jnp.concatenate(
            [
                embed - embed.mean(-1, keepdims=True),
                jnp.broadcast_to(
                    embed_bias[...] - embed_bias[...].mean(-1, keepdims=True),
                    (8, embed.shape[1]),
                ),
            ],
            axis=0,
        )
        gram[...] = lax.dot_general(
            centred, centred, (((1,), (1,)), ((), ())),
            precision=lax.Precision.HIGHEST, preferred_element_type=F32,
        ) * (1.0 / embed.shape[1])
        high, low = two_parts(gram[:lat, :lat])
        gram_split[:lat] = high
        gram_split[lat:] = low
        gained_high, gained_low = two_parts(centred * norm_gain[...])
        for which in range(3):
            loads[2 + which].wait()
            product = dot(gained_high, w_joined[which]) + dot(gained_low, w_joined[which])
            if which == 0:
                product = product * (HEAD_DIM**-0.5 * math.log2(math.e))
            blanks = jnp.zeros((product.shape[0], SLOT - HEAD_DIM), F32)
            for head in range(heads):
                piece = jnp.concatenate(
                    [product[:, head * HEAD_DIM : (head + 1) * HEAD_DIM], blanks], axis=1
                )
                slot = slice(head * SLOT, (head + 1) * SLOT)
                high, low = two_parts(piece[:lat])
                split[which, :lat, slot] = high
                split[which, lat:, slot] = low
                offsets[which, :, slot] = piece[lat:]

    def convolve(field, bias, filler):
        def tap(shift_t, shift_r, first):
            window = field[shift_t, pl.ds(shift_r, rows)].reshape(rows * width, chans)
            for shift_w in range(3):
                part = dot(window, taps[(shift_t * 3 + shift_r) * 3 + shift_w])
                if first:
                    acc[shift_w] = part
                else:
                    acc[shift_w] += part

        tap(1, 1, True)
        take_rows(field, 1)
        tap(1, 0, False)
        tap(1, 2, False)
        take_time(field, (0, 1))
        relay_rows(field)
        filler()
        take_time(field, (2,))
        tap(0, 1, False)
        tap(2, 1, False)
        take_rows(field, 0)
        take_rows(field, 2)

        @pl.loop(0, 2)
        def _(index):
            tap(0, 2 * index, False)
            tap(2, 2 * index, False)

        total = acc[1] + bias
        place = lax.broadcasted_iota(jnp.int32, total.shape, 0) % width
        total += jnp.where(place == 0, 0.0, pltpu.roll(acc[0], 1, 0))
        total += jnp.where(place == width - 1, 0.0, pltpu.roll(acc[2], rows * width - 1, 0))
        return total

    loads[1].wait()
    first = gelu(convolve(field_one, bias_one[...], merge_weights)).astype(BF16)
    field_two[1, 1 : rows + 1] = first.reshape(rows, width, chans)
    send_field(field_two)
    again = load(conv_two, taps, 5)
    again.start()
    again.wait()
    total = convolve(field_two, bias_two[...], lambda: None)
    own = field_two[1, 1 : rows + 1].reshape(rows * width, chans).astype(F32)
    second = (own + gelu(total)).astype(BF16)

    line = width // 2
    for block in range(rows // 2):
        upper = second[(2 * block) * width : (2 * block + 1) * width]
        lower = second[(2 * block + 1) * width : (2 * block + 2) * width]
        for col in range(2):
            pair[col] = dot(upper, patch_weight[0, col]) + dot(lower, patch_weight[1, col])
        patches = (
            pair[0, pl.ds(0, line, stride=2), :] + pair[1, pl.ds(1, line, stride=2), :]
            + patch_bias[...]
        ).astype(BF16)
        gathered[ba, pl.ds(pl.multiple_of(aa * tokens + block * line, line), line), :] = patches

    def along_aa(step):
        block = gathered.at[ba, pl.ds(pl.multiple_of(aa * tokens, tokens), tokens)]
        return pltpu.make_async_remote_copy(
            src_ref=block, dst_ref=block, send_sem=aa_send.at[step], recv_sem=aa_recv.at[step],
            device_id=((aa + step) % n_aa, ba), device_id_type=MESH,
        )

    def along_ba(step):
        return pltpu.make_async_remote_copy(
            src_ref=gathered.at[ba], dst_ref=gathered.at[ba],
            send_sem=ba_send.at[step], recv_sem=ba_recv.at[step],
            device_id=(aa, (ba + 2 * step) % n_ba), device_id_type=MESH,
        )

    def to_partner(step):
        block = gathered.at[(ba + n_ba - 2 * step) % n_ba]
        return pltpu.make_async_remote_copy(
            src_ref=block, dst_ref=block, send_sem=core_send.at[step], recv_sem=core_recv.at[step],
            device_id=(aa, partner), device_id_type=MESH,
        )

    slope = 2.0 * gram[lat : lat + 1, :lat]
    floor = gram[lat : lat + 1, lat : lat + 1]
    column = lax.broadcasted_iota(jnp.int32, (n_aa * tokens, SLOT), 1)

    def spread_of(latents, twice):
        bent = dot(twice, gram_split[...]) + slope
        power = (bent * latents.astype(F32)).sum(-1, keepdims=True) + floor
        return lax.rsqrt(jnp.maximum(power, 0.0) + 1e-05)

    def project(twice, scale, which):
        return ((dot(twice, split[which]) + offsets[which, :1]) * scale).astype(BF16)

    def take_block(block):
        latents = gathered[block]
        twice = jnp.concatenate([latents, latents], axis=1)
        scale = spread_of(latents, twice)
        projected_keys = project(twice, scale, 1)
        projected_values = project(twice, scale, 2)
        length = n_aa * tokens
        where = pl.ds(pl.multiple_of(block * length, length), length)
        for head in range(heads):
            keys[head, where] = projected_keys[:, head * SLOT : (head + 1) * SLOT]
            values[head, where] = jnp.where(
                column == HEAD_DIM,
                jnp.ones((), BF16),
                projected_values[:, head * SLOT : (head + 1) * SLOT],
            )
        mine = gathered[block, pl.ds(pl.multiple_of(aa * tokens, tokens), tokens)]
        twice = jnp.concatenate([mine, mine], axis=1)
        asked = project(twice, spread_of(mine, twice), 0)
        there = pl.ds(pl.multiple_of(block * tokens, tokens), tokens)
        for head in range(heads):
            queries[head, there] = asked[:, head * SLOT : (head + 1) * SLOT]

    for step in range(1, n_aa):
        along_aa(step).start()
    sent(field_one)
    sent(field_two)
    for step in range(1, n_aa):
        along_aa(step).wait_recv()
    for step in range(1, half):
        along_ba(step).start()
    to_partner(0).start()
    take_block(ba)
    to_partner(0).wait_recv()
    take_block(partner)

    @pl.loop(1, half)
    def _(step):
        along_ba(step).wait_recv()
        to_partner(step).start()
        take_block((ba + n_ba - 2 * step) % n_ba)

    @pl.loop(1, half)
    def _(step):
        to_partner(step).wait_recv()
        take_block((partner + n_ba - 2 * step) % n_ba)

    for step in range(1, n_aa):
        along_aa(step).wait_send()
    for step in range(1, half):
        along_ba(step).wait_send()
    for step in range(half):
        to_partner(step).wait_send()

    def share(dest):
        offset = (dest + n_ba - ba) % n_ba
        return pltpu.make_async_remote_copy(
            src_ref=shares.at[dest], dst_ref=arrived.at[ba],
            send_sem=share_send.at[offset], recv_sem=share_recv.at[offset],
            device_id=(aa, dest), device_id_type=MESH,
        )

    per_span = span // tokens
    spans = n_ba // per_span
    total = keys.shape[1]
    big = math.gcd(total, 4096)

    @pl.loop(0, spans)
    def _(step):
        at = (ba // per_span + 1 + step) % spans
        where = pl.ds(pl.multiple_of(at * span, span), span)

        def one_head(head, velocity):
            asked = queries[head, where]

            def one_big(index, state):
                best, accum = state
                for piece in range(big // chunk):
                    held = pl.ds(pl.multiple_of(index * big + piece * chunk, chunk), chunk)
                    scores = lax.dot_general(
                        asked, keys[head, held], (((1,), (1,)), ((), ())),
                        preferred_element_type=F32,
                    )
                    peak = jnp.maximum(best, scores.max(-1, keepdims=True))
                    probs = jnp.exp2(scores - peak).astype(BF16)
                    accum = accum * jnp.exp2(best - peak) + dot(probs, values[head, held])
                    best = peak
                return best, accum

            state = (jnp.full((span, 1), -jnp.inf, F32), jnp.zeros((span, SLOT), F32))
            if total == big:
                _, accum = one_big(0, state)
            else:
                _, accum = lax.fori_loop(0, total // big, one_big, state)
            attended = (accum[:, :HEAD_DIM] / accum[:, HEAD_DIM : HEAD_DIM + 1]).astype(BF16)
            rows = pl.ds(pl.multiple_of(head * HEAD_DIM, HEAD_DIM), HEAD_DIM)
            return velocity + dot(attended, w_velocity[rows])

        velocity = lax.fori_loop(0, heads, one_head, jnp.zeros((span, w_velocity.shape[1]), F32), unroll=2)
        for part in range(per_span):
            dest = at * per_span + part
            shares[dest] = velocity[part * tokens : (part + 1) * tokens].astype(BF16)

            @pl.when(dest != ba)
            def _():
                share(dest).start()

    summed = shares[ba].astype(F32)
    for offset in range(1, n_ba):
        share((ba + offset) % n_ba).wait_recv()
        summed += arrived[(ba + n_ba - offset) % n_ba].astype(F32)
    out[...] = summed
    for offset in range(1, n_ba):
        share((ba + offset) % n_ba).wait_send()


def on_device(
    n_aa, n_ba,
    feats, conv_one, bias_one, conv_two, bias_two, patch_weight, patch_bias,
    embed_weight, embed_bias, norm_gain, w_query, w_key, w_value, w_velocity,
):
    _, rows, width, chans = feats.shape
    lat = patch_bias.shape[0]
    features, qwidth = w_query.shape
    heads = qwidth // HEAD_DIM
    tokens = rows * width // 4
    total = n_ba * n_aa * tokens
    span = max(tokens, min(512, n_ba * tokens))
    chunk = math.gcd(total, 2048)
    vmem = pl.BlockSpec(memory_space=pltpu.VMEM)
    anywhere = pl.BlockSpec(memory_space=pl.ANY)
    dma = pltpu.SemaphoreType.DMA
    return pl.pallas_call(
        functools.partial(whole_kernel, n_aa, n_ba, span, chunk),
        out_shape=jax.ShapeDtypeStruct((tokens, lat), F32),
        in_specs=[anywhere, anywhere, vmem, anywhere] + [vmem] * 6 + [anywhere] * 3 + [vmem],
        out_specs=vmem,
        scratch_shapes=[
            pltpu.VMEM((3, rows + 2, width, chans), BF16),
            pltpu.VMEM((3, rows + 2, width, chans), BF16),
            pltpu.VMEM((27, chans, chans), BF16),
            pltpu.VMEM((3, features, qwidth), BF16),
            pltpu.VMEM((3, rows * width, chans), F32),
            pltpu.VMEM((2, width, lat), F32),
            pltpu.VMEM((n_ba, n_aa * tokens, lat), BF16),
            pltpu.VMEM((3, 2 * lat, heads * SLOT), BF16),
            pltpu.VMEM((3, 8, heads * SLOT), F32),
            pltpu.VMEM((2 * lat, lat), BF16),
            pltpu.VMEM((lat + 8, lat + 8), F32),
            pltpu.VMEM((heads, n_ba * tokens, SLOT), BF16),
            pltpu.VMEM((heads, total, SLOT), BF16),
            pltpu.VMEM((heads, total, SLOT), BF16),
            pltpu.VMEM((n_ba, tokens, lat), BF16),
            pltpu.VMEM((n_ba, tokens, lat), BF16),
            dma((6,)),
            dma((2, 2, 3)), dma((2, 2, 3)), dma((2, 3, 2)), dma((2, 3, 2)),
            dma((n_aa,)), dma((n_aa,)),
            dma((n_ba // 2,)), dma((n_ba // 2,)),
            dma((n_ba // 2,)), dma((n_ba // 2,)),
            dma((n_ba,)), dma((n_ba,)),
        ],
        compiler_params=pltpu.CompilerParams(
            collective_id=0, has_side_effects=True, vmem_limit_bytes=VMEM_BYTES
        ),
        name="whole",
    )(
        feats, conv_one.reshape(27, chans, chans), bias_one[None],
        conv_two.reshape(27, chans, chans), bias_two[None],
        patch_weight, patch_bias[None], embed_weight, embed_bias[None], norm_gain[None],
        w_query, w_key, w_value, w_velocity,
    )


def solution(mesh):
    return jax.shard_map(
        functools.partial(on_device, mesh.shape["aa"], mesh.shape["ba"]),
        mesh=mesh,
        in_specs=(
            P("aa", "ba", None, None), P(), P(), P(), P(), P(), P(), P(), P(), P(),
            P(None, "ba"), P(None, "ba"), P(None, "ba"), P("ba", None),
        ),
        out_specs=P(("aa", "ba"), None),
        check_vma=False,
    )
```

profile of v0, /device:TPU:0, one launch (start us, length us, event | category | flops | bytes accessed | tf_op | source)
XLA Modules:
  0.0 72.0 jit_solution(16284078765233630472)
XLA Ops:
  0.0 70.6 %whole.1 = f32[128,128]{1,0:T(8,128)} custom-call(bf16[1,4,128,256]{3,2,1,0:T(8,128)(2,1)} %feats.1, bf16[27,256,256]{2,1,0:T(8,128)(2,1)} %bitcast.7, f32[1,256]{1,0:T(1,128)} %bitcast.11, bf16[27,256,256]{2,1,0:T(8,128)(2,1)} %bitcast.8, f32[1,256]{1,0:T(1,128)} %bitcast.12, bf16[2,2,256,128]{3,2,1,0:T(8,128)(2,1)} %patch_weight.1, f32[1,128]{1,0:T(1,128)} %bitcast.13, ...), custom_call_target="tpu_custom_call" | custom-call | tf_op jit(solution)/shard_map/whole/pallas_call | solution.py:420
  70.6 1.5 %copy.16 = f32[128,128]{1,0:T(8,128)} copy(f32[128,128]{1,0:T(8,128)} %whole.1) | data formatting | bytes 131072
where the time goes:
time: 72.3 us; the launch traced here: 72 us
  Pallas kernels  70.6 us (98%)
  local copies, waits for them, and re-layouts  1.47 us (2%)
    pallas_call x1, Pallas kernels, on_device(): pl.pallas_call(functools.partial(whole_kernel, n_aa, n_ba, span, chunk),...  70.6 us
    unnamed x1, local copies, waits for them, and re-layouts  1.47 us

commit v1 on v0

v1 whole, which is shorter than its diff:
```python
import functools
import math

import jax
import jax.numpy as jnp
from jax import lax
from jax.experimental import pallas as pl
from jax.experimental.pallas import tpu as pltpu
from jax.sharding import PartitionSpec as P

HEAD_DIM = 64
SLOT = 128
MESH = pl.DeviceIdType.MESH
GROUP = 2
LOOK = 2
STACK = HEAD_DIM + 16
F32 = jnp.float32
BF16 = jnp.bfloat16
VMEM_BYTES = 67043328


def dot(left, right):
    return jnp.dot(left, right, preferred_element_type=F32)


def two_parts(value):
    high = value.astype(BF16)
    return high, (value - high.astype(F32)).astype(BF16)


def gelu(value):
    return 0.5 * value * (1.0 + lax.erf(value * (0.5**0.5)))


def whole_kernel(
    n_aa, n_ba, span, chunk,
    feats, conv_one, bias_one, conv_two, bias_two, patch_weight, patch_bias,
    embed_weight, embed_bias, norm_gain, w_query, w_key, w_value, w_velocity,
    out,
    field, taps, w_joined, outgoing, incoming, acc, pair, gathered, split, offsets, turned, lift,
    gram_split, gram, queries, keys, values, attended, shares, arrived,
    load_sem, aa_side_send, aa_side_recv, ba_side_send, ba_side_recv,
    token_recv, aa_send, ba_send, core_send, share_send, share_recv,
):
    aa, ba = lax.axis_index("aa"), lax.axis_index("ba")
    _, rows, width, chans = feats.shape
    partner = ba + 1 - 2 * (ba % 2)
    half = n_ba // 2
    width_q = w_query.shape[1]
    heads = width_q // HEAD_DIM
    tokens = rows * width // 4
    lat = patch_bias.shape[1]

    def load(source, target, at):
        return pltpu.make_async_copy(source, target, load_sem.at[at])

    loads = [
        load(feats.at[0], field.at[0, 1, pl.ds(1, rows)], 0),
        load(w_query, w_joined.at[0], 1),
        load(w_key, w_joined.at[1], 2),
        load(w_value, w_joined.at[2], 3),
    ]
    kernels = [
        [load(source.at[at], taps.at[which, :, :, pl.ds(column * chans, chans)], 4 + 3 * which + at)
         for at, column in enumerate((0, 2, 1))]
        for which, source in enumerate((conv_one, conv_two))
    ]
    loads[0].start()
    for at in (0, 2, 1):
        kernels[0][at].start()
    for one in loads[1:]:
        one.start()
    for at in (0, 2, 1):
        kernels[1][at].start()

    def aa_there(side):
        return aa > 0 if side == -1 else aa < n_aa - 1

    def ba_there(side):
        return ba > 0 if side == -1 else ba < n_ba - 1

    barrier = pltpu.get_barrier_semaphore()
    for step in range(1, n_aa):
        pl.semaphore_signal(
            barrier, inc=1, device_id=((aa + step) % n_aa, ba), device_id_type=MESH
        )
    for step in range(1, n_ba):
        pl.semaphore_signal(
            barrier, inc=1, device_id=(aa, (ba + step) % n_ba), device_id_type=MESH
        )

    edges, middle, both = 0, 1, 2
    parts = (slice(0, 2), slice(2, rows))

    def along_time(which, side, part):
        at = (which, (side + 1) // 2, part)
        here = (which, (side + 1) // 2, parts[part])
        return pltpu.make_async_remote_copy(
            src_ref=outgoing.at[here], dst_ref=incoming.at[here],
            send_sem=aa_side_send.at[at], recv_sem=aa_side_recv.at[at],
            device_id=(aa + side, ba), device_id_type=MESH,
        )

    def along_rows(which, side):
        source, target = (rows, 0) if side == 1 else (1, rows + 1)
        at = (which, (side + 1) // 2)
        return pltpu.make_async_remote_copy(
            src_ref=field.at[which, 1, source], dst_ref=field.at[which, 1, target],
            send_sem=ba_side_send.at[at], recv_sem=ba_side_recv.at[at],
            device_id=(aa, ba + side), device_id_type=MESH,
        )

    def send_rows(which):
        for side in (-1, 1):
            pl.when(ba_there(side))(along_rows(which, side).start)

    def take_rows(which):
        for side in (-1, 1):
            pl.when(ba_there(-side))(along_rows(which, side).wait_recv)
        shift(which, 0, 1)
        shift(which, rows + 1, 1)

    def take_time(which, part):
        for side in (-1, 1):
            pl.when(aa_there(-side))(along_time(which, side, part).wait_recv)

    def sent(which):
        for side in (-1, 1):
            pl.when(ba_there(side))(along_rows(which, side).wait_send)
            for part in (edges, middle):
                pl.when(aa_there(side))(along_time(which, side, part).wait_send)

    def blank():
        line = jnp.zeros((width, chans), BF16)
        for which in range(2):
            for side, row in ((-1, 0), (1, rows + 1)):
                @pl.when(jnp.logical_not(ba_there(side)))
                def _():
                    field[which, 1, row] = line

                @pl.when(jnp.logical_not(aa_there(side)))
                def _():
                    for at in range(rows):
                        incoming[which, (1 - side) // 2, at] = line

    def shift(which, row, count):
        here = pl.ds(row, count)
        held = field[which, 1, here].reshape(count * width, chans).astype(F32)
        place = lax.broadcasted_iota(jnp.int32, held.shape, 0) % width
        before = jnp.where(place == 0, 0.0, pltpu.roll(held, 1, 0))
        after = jnp.where(place == width - 1, 0.0, pltpu.roll(held, count * width - 1, 0))
        field[which, 0, here] = before.astype(BF16).reshape(count, width, chans)
        field[which, 2, here] = after.astype(BF16).reshape(count, width, chans)

    def stack(which, part):
        def window(shift_r, shift_w):
            if part == middle:
                held = field[which, shift_w, pl.ds(1 + shift_r, rows - 2)]
                return held.reshape((rows - 2) * width, chans)
            if part == both:
                return field[which, shift_w, pl.ds(shift_r, rows)].reshape(rows * width, chans)
            return jnp.concatenate(
                [field[which, shift_w, shift_r], field[which, shift_w, rows - 1 + shift_r]], axis=0
            )

        return jnp.concatenate(
            [window(shift_r, shift_w) for shift_r in range(3) for shift_w in range(3)], axis=1
        )

    def send_time(which, part):
        made = dot(
            stack(which, part), taps[which, :, :, : 2 * chans].reshape(9 * chans, 2 * chans)
        ).astype(BF16)
        for side, column in ((-1, chans), (1, 0)):
            outgoing[which, (side + 1) // 2, parts[part]] = made[
                :, column : column + chans
            ].reshape(-1, width, chans)
            pl.when(aa_there(side))(along_time(which, side, part).start)

    def keep(which):
        acc[...] = dot(
            stack(which, both), taps[which, :, :, 2 * chans :].reshape(9 * chans, chans)
        ).reshape(rows, width, chans)

    def activate(which, part, bias):
        here = parts[part]
        kept = acc[1 : rows - 1] if part == middle else jnp.concatenate(
            [acc[:1], acc[rows - 1 :]], axis=0
        )
        total = kept + incoming[which, 0, here].astype(F32)
        total += incoming[which, 1, here].astype(F32)
        return gelu(total.reshape(-1, chans) + bias)

    blank()
    loads[0].wait()
    shift(0, 1, rows)
    pl.semaphore_wait(barrier, n_aa - 1 + n_ba - 1)
    send_rows(0)
    kernels[0][0].wait()
    kernels[0][2].wait()
    send_time(0, middle)
    take_rows(0)
    send_time(0, edges)

    def merge_weights():
        embed = embed_weight[...].astype(F32)
        centred = jnp.concatenate(
            [
                embed - embed.mean(-1, keepdims=True),
                jnp.broadcast_to(
                    embed_bias[...] - embed_bias[...].mean(-1, keepdims=True),
                    (8, embed.shape[1]),
                ),
            ],
            axis=0,
        )
        gram[...] = lax.dot_general(
            centred, centred, (((1,), (1,)), ((), ())),
            precision=lax.Precision.HIGHEST, preferred_element_type=F32,
        ) * (1.0 / embed.shape[1])
        high, low = two_parts(gram[:lat, :lat])
        gram_split[:lat] = high
        gram_split[lat:] = low
        turned[width_q : width_q + lat, :lat] = high
        turned[width_q : width_q + lat, lat:] = low
        across = lax.broadcasted_iota(jnp.int32, (lat, 2 * lat), 1)
        down = lax.broadcasted_iota(jnp.int32, (lat, 2 * lat), 0)
        turned[width_q + lat :] = (across == down).astype(BF16)
        gained = jnp.concatenate(two_parts(centred * norm_gain[...]), axis=0)
        for which in range(3):
            loads[1 + which].wait()
            product = dot(gained, w_joined[which])
            product = product[: lat + 8] + product[lat + 8 :]
            if which == 2:
                high, low = two_parts(product[:lat].T)
                turned[:width_q, :lat] = high
                turned[:width_q, lat:] = low
                lift[...] = product[lat:].T
                continue
            if which == 0:
                product = product * (HEAD_DIM**-0.5 * math.log2(math.e))
            blanks = jnp.zeros((product.shape[0], SLOT - HEAD_DIM), F32)
            for head in range(heads):
                piece = jnp.concatenate(
                    [product[:, head * HEAD_DIM : (head + 1) * HEAD_DIM], blanks], axis=1
                )
                slot = slice(head * SLOT, (head + 1) * SLOT)
                high, low = two_parts(piece[:lat])
                split[which, :lat, slot] = high
                split[which, lat:, slot] = low
                offsets[which, :, slot] = piece[lat:]

    kernels[0][1].wait()
    keep(0)
    merge_weights()
    take_time(0, middle)
    take_time(0, edges)
    first = activate(0, edges, bias_one[...]).astype(BF16)
    field[1, 1, 1] = first[:width]
    field[1, 1, rows] = first[width:]
    send_rows(1)
    first = activate(0, middle, bias_one[...]).astype(BF16)
    field[1, 1, 2:rows] = first.reshape(-1, width, chans)
    shift(1, 1, rows)
    for at in (0, 2, 1):
        kernels[1][at].wait()
    send_time(1, middle)
    take_rows(1)
    send_time(1, edges)
    keep(1)

    def finish(part):
        here = field[1, 1, 2:rows] if part == middle else jnp.concatenate(
            [field[1, 1, 1], field[1, 1, rows]], axis=0
        )
        own = here.reshape(-1, chans).astype(F32)
        return (own + activate(1, part, bias_two[...])).astype(BF16)

    take_time(1, middle)
    inner = finish(middle)
    take_time(1, edges)
    outer = finish(edges)
    lines = [outer[:width]]
    lines += [inner[at * width : (at + 1) * width] for at in range(rows - 2)]
    lines += [outer[width:]]

    line = width // 2
    for block in range(rows // 2):
        for col in range(2):
            pair[col] = dot(lines[2 * block], patch_weight[0, col]) + dot(
                lines[2 * block + 1], patch_weight[1, col]
            )
        patches = (
            pair[0, pl.ds(0, line, stride=2), :] + pair[1, pl.ds(1, line, stride=2), :]
            + patch_bias[...]
        ).astype(BF16)
        gathered[aa, ba, pl.ds(block * line, line), :] = patches

    turn = jnp.where(aa < n_aa // 2, 1, n_aa - 1)
    values[:, HEAD_DIM:] = jnp.ones((heads, values.shape[1] - HEAD_DIM, values.shape[2]), BF16)

    def frame_of(step):
        return (aa + turn * step) % n_aa

    def piece(frame, block, send_sem, to_aa, to_ba):
        here = gathered.at[frame, block]
        return pltpu.make_async_remote_copy(
            src_ref=here, dst_ref=here, send_sem=send_sem, recv_sem=token_recv.at[frame, block],
            device_id=(to_aa, to_ba), device_id_type=MESH,
        )

    def along_aa(step):
        return piece(aa, ba, aa_send.at[step], (aa + n_aa - turn * step + n_aa * n_aa) % n_aa, ba)

    def along_ba(step, hop):
        return piece(frame_of(step), ba, ba_send.at[step, hop], aa, (ba + 2 * hop) % n_ba)

    def to_partner(step, hop):
        block = (ba + n_ba - 2 * hop) % n_ba
        return piece(frame_of(step), block, core_send.at[step, hop], aa, partner)

    def landed(frame, block):
        piece(frame, block, aa_send.at[0], aa, partner).wait_recv()

    slope = 2.0 * gram[lat : lat + 1, :lat]
    slope_down = 2.0 * gram[:lat, lat : lat + 1]
    floor = gram[lat : lat + 1, lat : lat + 1]

    def take_pair(step, hop, with_queries):
        frame = frame_of(step)
        block = ((ba + n_ba - 2 * hop) % n_ba) // 2
        latents = gathered[frame, pl.ds(2 * block, 2)].reshape(2 * tokens, lat)
        twice = jnp.concatenate([latents, latents], axis=1)
        bent = dot(twice, gram_split[...]) + slope
        power = (bent * latents.astype(F32)).sum(-1, keepdims=True) + floor
        scale = lax.rsqrt(jnp.maximum(power, 0.0) + 1e-05)
        at = pl.multiple_of((frame * half + block) * 2 * tokens, 2 * tokens)
        projected = ((dot(twice, split[1]) + offsets[1, :1]) * scale).astype(BF16)
        for head in range(heads):
            keys[head, pl.ds(at, 2 * tokens)] = projected[:, head * SLOT : (head + 1) * SLOT]
        down = lax.dot_general(
            turned[...], twice, (((1,), (1,)), ((), ())), preferred_element_type=F32
        )
        bent = (down[width_q : width_q + lat] + slope_down) * down[width_q + lat :]
        power = bent.sum(0, keepdims=True) + floor
        scale_down = lax.rsqrt(jnp.maximum(power, 0.0) + 1e-05)
        flipped = ((down[:width_q] + lift[:, :1]) * scale_down).astype(BF16)
        for head in range(heads):
            values[head, :HEAD_DIM, pl.ds(at, 2 * tokens)] = flipped[
                head * HEAD_DIM : (head + 1) * HEAD_DIM
            ]
        if with_queries:
            asked = ((dot(twice, split[0]) + offsets[0, :1]) * scale).astype(BF16)
            there = pl.ds(pl.multiple_of(block * 2 * tokens, 2 * tokens), 2 * tokens)
            for head in range(heads):
                queries[head, there] = asked[:, head * SLOT : (head + 1) * SLOT]

    def pass_on(step):
        for hop in range(1, half):
            along_ba(step, hop).start()
        to_partner(step, 0).start()

    def frame_step(step, first, with_queries):
        @pl.loop(1, half)
        def _(hop):
            landed(frame_of(step), (ba + n_ba - 2 * hop) % n_ba)
            to_partner(step, hop).start()

        @pl.when(step + 2 < n_aa)
        def _():
            landed(frame_of(step + 2), ba)
            pass_on(step + 2)

        @pl.loop(first, half)
        def _(hop):
            landed(frame_of(step), (partner + n_ba - 2 * hop) % n_ba)
            take_pair(step, hop, with_queries)

    for step in range(1, n_aa):
        along_aa(step).start()
    pass_on(0)
    sent(0)
    sent(1)
    landed(aa, partner)
    take_pair(0, 0, True)
    landed(frame_of(1), ba)
    pass_on(1)
    frame_step(0, 1, True)

    @pl.loop(1, n_aa)
    def _(step):
        frame_step(step, 0, False)

    for step in range(1, n_aa):
        along_aa(step).wait_send()

    @pl.loop(0, n_aa)
    def _(step):
        to_partner(step, 0).wait_send()

        @pl.loop(1, half)
        def _(hop):
            along_ba(step, hop).wait_send()
            to_partner(step, hop).wait_send()

    def share(dest):
        offset = (dest + n_ba - ba) % n_ba
        return pltpu.make_async_remote_copy(
            src_ref=shares.at[dest], dst_ref=arrived.at[ba],
            send_sem=share_send.at[offset], recv_sem=share_recv.at[offset],
            device_id=(aa, dest), device_id_type=MESH,
        )

    per_span = span // tokens
    spans = n_ba // per_span
    total = keys.shape[1]
    big = math.gcd(total, 4096)

    @pl.loop(0, spans)
    def _(step):
        at = (ba // per_span + 1 + step) % spans
        where = pl.ds(pl.multiple_of(at * span, span), span)

        def sweep(group, asked, base, state):
            order = [(each, part) for each in range(len(asked)) for part in range(big // chunk)]

            def held(part):
                return pl.ds(pl.multiple_of(base + part * chunk, chunk), chunk)

            def score(each, part):
                return lax.dot_general(
                    keys[group + each, held(part)], asked[each], (((1,), (1,)), ((), ())),
                    preferred_element_type=F32,
                )

            def gather(each, part, shrink, probs):
                best, accum = state[each]
                added = dot(values[group + each, :, held(part)], probs)
                return added if shrink is None else accum * shrink + added

            ahead = [score(*one) for one in order[:LOOK]]
            late = None
            for index, (each, part) in enumerate(order):
                if index + LOOK < len(order):
                    ahead.append(score(*order[index + LOOK]))
                scores, ahead[index] = ahead[index], None
                best, accum = state[each]
                peak = scores.max(0, keepdims=True)
                shrink = None
                if best is not None:
                    peak = jnp.maximum(best, peak)
                    shrink = jnp.exp2(best - peak)
                probs = jnp.exp2(scores - peak).astype(BF16)
                if late is not None:
                    state[late[0]] = (state[late[0]][0], gather(*late))
                state[each] = (peak, state[each][1])
                late = (each, part, shrink, probs)
            state[late[0]] = (state[late[0]][0], gather(*late))
            return state

        @pl.loop(0, heads // GROUP)
        def _(index):
            group = index * GROUP
            asked = [queries[group + each, where] for each in range(GROUP)]
            if total == big:
                state = sweep(group, asked, 0, [(None, None)] * GROUP)
            else:
                empty = (jnp.full((1, span), -jnp.inf, F32), jnp.zeros((values.shape[1], span), F32))

                def one_big(index, state):
                    return tuple(sweep(group, asked, index * big, list(state)))

                state = lax.fori_loop(0, total // big, one_big, (empty,) * GROUP)
            for each in range(GROUP):
                accum = state[each][1]
                rows = pl.ds(pl.multiple_of((group + each) * HEAD_DIM, HEAD_DIM), HEAD_DIM)
                attended[rows] = (accum[:HEAD_DIM] / accum[HEAD_DIM : HEAD_DIM + 1]).astype(BF16)

        velocity = lax.dot_general(
            w_velocity[...], attended[...], (((0,), (0,)), ((), ())), preferred_element_type=F32
        )
        for part in range(per_span):
            dest = at * per_span + part
            shares[dest] = velocity[:, part * tokens : (part + 1) * tokens].astype(BF16)

            @pl.when(dest != ba)
            def _():
                share(dest).start()

    summed = shares[ba].astype(F32)
    for offset in range(1, n_ba):
        share((ba + offset) % n_ba).wait_recv()
        summed += arrived[(ba + n_ba - offset) % n_ba].astype(F32)
    out[...] = summed.T
    for offset in range(1, n_ba):
        share((ba + offset) % n_ba).wait_send()


def on_device(
    n_aa, n_ba,
    feats, conv_one, bias_one, conv_two, bias_two, patch_weight, patch_bias,
    embed_weight, embed_bias, norm_gain, w_query, w_key, w_value, w_velocity,
):
    _, rows, width, chans = feats.shape
    lat = patch_bias.shape[0]
    features, qwidth = w_query.shape
    heads = qwidth // HEAD_DIM
    tokens = rows * width // 4
    total = n_ba * n_aa * tokens
    span = max(tokens, min(512, n_ba * tokens))
    chunk = math.gcd(total, 256)
    vmem = pl.BlockSpec(memory_space=pltpu.VMEM)
    anywhere = pl.BlockSpec(memory_space=pl.ANY)
    dma = pltpu.SemaphoreType.DMA
    return pl.pallas_call(
        functools.partial(whole_kernel, n_aa, n_ba, span, chunk),
        out_shape=jax.ShapeDtypeStruct((tokens, lat), F32),
        in_specs=[anywhere, anywhere, vmem, anywhere] + [vmem] * 6 + [anywhere] * 3 + [vmem],
        out_specs=vmem,
        scratch_shapes=[
            pltpu.VMEM((2, 3, rows + 2, width, chans), BF16),
            pltpu.VMEM((2, 9, chans, 3 * chans), BF16),
            pltpu.VMEM((3, features, qwidth), BF16),
            pltpu.VMEM((2, 2, rows, width, chans), BF16),
            pltpu.VMEM((2, 2, rows, width, chans), BF16),
            pltpu.VMEM((rows, width, chans), F32),
            pltpu.VMEM((2, width, lat), F32),
            pltpu.VMEM((n_aa, n_ba, tokens, lat), BF16),
            pltpu.VMEM((2, 2 * lat, heads * SLOT), BF16),
            pltpu.VMEM((2, 8, heads * SLOT), F32),
            pltpu.VMEM((qwidth + 2 * lat, 2 * lat), BF16),
            pltpu.VMEM((qwidth, 8), F32),
            pltpu.VMEM((2 * lat, lat), BF16),
            pltpu.VMEM((lat + 8, lat + 8), F32),
            pltpu.VMEM((heads, n_ba * tokens, SLOT), BF16),
            pltpu.VMEM((heads, total, SLOT), BF16),
            pltpu.VMEM((heads, STACK, total), BF16),
            pltpu.VMEM((qwidth, span), BF16),
            pltpu.VMEM((n_ba, lat, tokens), BF16),
            pltpu.VMEM((n_ba, lat, tokens), BF16),
            dma((10,)),
            dma((2, 2, 2)), dma((2, 2, 2)), dma((2, 2)), dma((2, 2)),
            dma((n_aa, n_ba)), dma((n_aa,)), dma((n_aa, n_ba // 2)), dma((n_aa, n_ba // 2)),
            dma((n_ba,)), dma((n_ba,)),
        ],
        compiler_params=pltpu.CompilerParams(
            collective_id=0, has_side_effects=True, vmem_limit_bytes=VMEM_BYTES
        ),
        name="whole",
    )(
        feats, conv_one.reshape(3, 9, chans, chans), bias_one[None],
        conv_two.reshape(3, 9, chans, chans), bias_two[None],
        patch_weight, patch_bias[None], embed_weight, embed_bias[None], norm_gain[None],
        w_query, w_key, w_value, w_velocity,
    )


def solution(mesh):
    return jax.shard_map(
        functools.partial(on_device, mesh.shape["aa"], mesh.shape["ba"]),
        mesh=mesh,
        in_specs=(
            P("aa", "ba", None, None), P(), P(), P(), P(), P(), P(), P(), P(), P(),
            P(None, "ba"), P(None, "ba"), P(None, "ba"), P("ba", None),
        ),
        out_specs=P(("aa", "ba"), None),
        check_vma=False,
    )
```

time: 72.3 us -> 64.4 us (0.89)
  Pallas kernels: 70.6 us -> 62.8 us
    pallas_call x1, Pallas kernels: 70.6 us -> 62.8 us  [on_device(): pl.pallas_call(functools.partial(whole_kernel, n_aa, n_ba, span, chunk),...]
where the time goes in v1:
time: 64.4 us; the launch traced here: 64.3 us
  Pallas kernels  62.8 us (98%)
  local copies, waits for them, and re-layouts  1.47 us (2%)
    pallas_call x1, Pallas kernels, on_device(): pl.pallas_call(functools.partial(whole_kernel, n_aa, n_ba, span, chunk),...  62.8 us
    unnamed x1, local copies, waits for them, and re-layouts  1.47 us

profile of v1, /device:TPU:0, one launch (start us, length us, event | category | flops | bytes accessed | tf_op | source)
XLA Modules:
  0.0 64.3 jit_solution(8655613235955861411)
XLA Ops:
  0.0 62.8 %whole.1 = f32[128,128]{1,0:T(8,128)} custom-call(bf16[1,4,128,256]{3,2,1,0:T(8,128)(2,1)} %feats.1, bf16[3,9,256,256]{3,2,1,0:T(8,128)(2,1)} %bitcast.7, f32[1,256]{1,0:T(1,128)} %bitcast.11, bf16[3,9,256,256]{3,2,1,0:T(8,128)(2,1)} %bitcast.8, f32[1,256]{1,0:T(1,128)} %bitcast.12, bf16[2,2,256,128]{3,2,1,0:T(8,128)(2,1)} %patch_weight.1, ...), custom_call_target="tpu_custom_call" | custom-call | tf_op jit(solution)/shard_map/whole/pallas_call | solution.py:515
  62.8 1.5 %copy.16 = f32[128,128]{1,0:T(8,128)} copy(f32[128,128]{1,0:T(8,128)} %whole.1) | data formatting | bytes 131072

commit v2 on v1

--- a/solution.py
+++ b/solution.py
@@ -33,13 +33,14 @@
 
 
 def whole_kernel(
-    n_aa, n_ba, span, chunk,
-    feats, conv_one, bias_one, conv_two, bias_two, patch_weight, patch_bias,
-    embed_weight, embed_bias, norm_gain, w_query, w_key, w_value, w_velocity,
+    n_aa, n_ba, span, narrow, chunk,
+    feats, conv_one, bias_one_in, conv_two, bias_two_in, patch_weight_in, patch_bias_in,
+    embed_weight_in, embed_bias_in, norm_gain_in, w_query, w_key, w_value, w_velocity_in,
     out,
-    field, taps, w_joined, outgoing, incoming, acc, pair, gathered, split, offsets, turned, lift,
+    bias_one, bias_two, patch_weight, patch_bias, embed_weight, embed_bias, norm_gain, w_velocity, gained,
+    field, taps, w_joined, outgoing, incoming, acc, pair, gathered, split_query, query_offset, split_key, key_offset, turned, lift,
     gram_split, gram, queries, keys, values, attended, shares, arrived,
-    load_sem, aa_side_send, aa_side_recv, ba_side_send, ba_side_recv,
+    load_sem, small_sem, aa_side_send, aa_side_recv, ba_side_send, ba_side_recv,
     token_recv, aa_send, ba_send, core_send, share_send, share_recv,
 ):
     aa, ba = lax.axis_index("aa"), lax.axis_index("ba")
@@ -65,13 +66,25 @@
          for at, column in enumerate((0, 2, 1))]
         for which, source in enumerate((conv_one, conv_two))
     ]
+    small = [
+        pltpu.make_async_copy(source, target, small_sem.at[at])
+        for at, (source, target) in enumerate((
+            (bias_one_in, bias_one), (embed_weight_in, embed_weight), (embed_bias_in, embed_bias),
+            (norm_gain_in, norm_gain), (bias_two_in, bias_two), (patch_weight_in, patch_weight),
+            (patch_bias_in, patch_bias), (w_velocity_in, w_velocity),
+        ))
+    ]
     loads[0].start()
     for at in (0, 2, 1):
         kernels[0][at].start()
+    for one in small[:4]:
+        one.start()
     for one in loads[1:]:
         one.start()
     for at in (0, 2, 1):
         kernels[1][at].start()
+    for one in small[4:]:
+        one.start()
 
     def aa_there(side):
         return aa > 0 if side == -1 else aa < n_aa - 1
@@ -202,7 +215,9 @@
     take_rows(0)
     send_time(0, edges)
 
-    def merge_weights():
+    def merge_gram():
+        for one in small[:4]:
+            one.wait()
         embed = embed_weight[...].astype(F32)
         centred = jnp.concatenate(
             [
@@ -226,48 +241,60 @@
         across = lax.broadcasted_iota(jnp.int32, (lat, 2 * lat), 1)
         down = lax.broadcasted_iota(jnp.int32, (lat, 2 * lat), 0)
         turned[width_q + lat :] = (across == down).astype(BF16)
-        gained = jnp.concatenate(two_parts(centred * norm_gain[...]), axis=0)
-        for which in range(3):
-            loads[1 + which].wait()
-            product = dot(gained, w_joined[which])
-            product = product[: lat + 8] + product[lat + 8 :]
-            if which == 2:
-                high, low = two_parts(product[:lat].T)
-                turned[:width_q, :lat] = high
-                turned[:width_q, lat:] = low
-                lift[...] = product[lat:].T
-                continue
-            if which == 0:
-                product = product * (HEAD_DIM**-0.5 * math.log2(math.e))
-            blanks = jnp.zeros((product.shape[0], SLOT - HEAD_DIM), F32)
+        gained[...] = jnp.concatenate(two_parts(centred * norm_gain[...]), axis=0)
+
+    def merge(which):
+        loads[1 + which].wait()
+        product = dot(gained[...], w_joined[which])
+        product = product[: lat + 8] + product[lat + 8 :]
+        if which == 0:
+            product = product * (HEAD_DIM**-0.5 * math.log2(math.e))
+            blanks = jnp.zeros((product.shape[0], HEAD_DIM), F32)
             for head in range(heads):
-                piece = jnp.concatenate(
-                    [product[:, head * HEAD_DIM : (head + 1) * HEAD_DIM], blanks], axis=1
-                )
+                piece = product[:, head * HEAD_DIM : (head + 1) * HEAD_DIM]
+                ordered = (blanks, piece) if head % 2 else (piece, blanks)
+                piece = jnp.concatenate(ordered, axis=1)
                 slot = slice(head * SLOT, (head + 1) * SLOT)
                 high, low = two_parts(piece[:lat])
-                split[which, :lat, slot] = high
-                split[which, lat:, slot] = low
-                offsets[which, :, slot] = piece[lat:]
+                split_query[:lat, slot] = high
+                split_query[lat:, slot] = low
+                query_offset[:, slot] = piece[lat:]
+        elif which == 1:
+            high, low = two_parts(product[:lat])
+            split_key[:lat] = high
+            split_key[lat:] = low
+            key_offset[...] = product[lat:]
+        else:
+            high, low = two_parts(product[:lat].T)
+            turned[:width_q, :lat] = high
+            turned[:width_q, lat:] = low
+            lift[...] = product[lat:].T
 
     kernels[0][1].wait()
     keep(0)
-    merge_weights()
+    merge_gram()
+    merge(2)
     take_time(0, middle)
+    first = activate(0, middle, bias_one[...]).astype(BF16)
+    field[1, 1, 2:rows] = first.reshape(-1, width, chans)
+    shift(1, 2, rows - 2)
     take_time(0, edges)
     first = activate(0, edges, bias_one[...]).astype(BF16)
     field[1, 1, 1] = first[:width]
     field[1, 1, rows] = first[width:]
     send_rows(1)
-    first = activate(0, middle, bias_one[...]).astype(BF16)
-    field[1, 1, 2:rows] = first.reshape(-1, width, chans)
-    shift(1, 1, rows)
+    shift(1, 1, 1)
+    shift(1, rows, 1)
     for at in (0, 2, 1):
         kernels[1][at].wait()
     send_time(1, middle)
+    merge(1)
     take_rows(1)
     send_time(1, edges)
     keep(1)
+    merge(0)
+    for one in small[4:]:
+        one.wait()
 
     def finish(part):
         here = field[1, 1, 2:rows] if part == middle else jnp.concatenate(
@@ -296,11 +323,14 @@
         ).astype(BF16)
         gathered[aa, ba, pl.ds(block * line, line), :] = patches
 
-    turn = jnp.where(aa < n_aa // 2, 1, n_aa - 1)
     values[:, HEAD_DIM:] = jnp.ones((heads, values.shape[1] - HEAD_DIM, values.shape[2]), BF16)
 
+    flanked = jnp.minimum(aa, n_aa - 1 - aa)
+    toward = jnp.where(aa < n_aa - 1 - aa, 1, -1)
+
     def frame_of(step):
-        return (aa + turn * step) % n_aa
+        near = (1 - 2 * ((step + 1) % 2)) * ((step + 1) // 2)
+        return aa + jnp.where(step <= 2 * flanked, near, toward * (step - flanked))
 
     def piece(frame, block, send_sem, to_aa, to_ba):
         here = gathered.at[frame, block]
@@ -310,7 +340,7 @@
         )
 
     def along_aa(step):
-        return piece(aa, ba, aa_send.at[step], (aa + n_aa - turn * step + n_aa * n_aa) % n_aa, ba)
+        return piece(aa, ba, aa_send.at[step], frame_of(step), ba)
 
     def along_ba(step, hop):
         return piece(frame_of(step), ba, ba_send.at[step, hop], aa, (ba + 2 * hop) % n_ba)
@@ -326,18 +356,18 @@
     slope_down = 2.0 * gram[:lat, lat : lat + 1]
     floor = gram[lat : lat + 1, lat : lat + 1]
 
-    def take_pair(step, hop, with_queries):
+    def take_pairs(step, hops, with_queries):
         frame = frame_of(step)
-        block = ((ba + n_ba - 2 * hop) % n_ba) // 2
-        latents = gathered[frame, pl.ds(2 * block, 2)].reshape(2 * tokens, lat)
+        blocks = [((ba + n_ba - 2 * hop) % n_ba) // 2 for hop in hops]
+        size = 2 * tokens
+        latents = jnp.concatenate(
+            [gathered[frame, pl.ds(2 * block, 2)].reshape(size, lat) for block in blocks], axis=0
+        )
         twice = jnp.concatenate([latents, latents], axis=1)
         bent = dot(twice, gram_split[...]) + slope
         power = (bent * latents.astype(F32)).sum(-1, keepdims=True) + floor
         scale = lax.rsqrt(jnp.maximum(power, 0.0) + 1e-05)
-        at = pl.multiple_of((frame * half + block) * 2 * tokens, 2 * tokens)
-        projected = ((dot(twice, split[1]) + offsets[1, :1]) * scale).astype(BF16)
-        for head in range(heads):
-            keys[head, pl.ds(at, 2 * tokens)] = projected[:, head * SLOT : (head + 1) * SLOT]
+        projected = ((dot(twice, split_key[...]) + key_offset[:1]) * scale).astype(BF16)
         down = lax.dot_general(
             turned[...], twice, (((1,), (1,)), ((), ())), preferred_element_type=F32
         )
@@ -345,51 +375,71 @@
         power = bent.sum(0, keepdims=True) + floor
         scale_down = lax.rsqrt(jnp.maximum(power, 0.0) + 1e-05)
         flipped = ((down[:width_q] + lift[:, :1]) * scale_down).astype(BF16)
-        for head in range(heads):
-            values[head, :HEAD_DIM, pl.ds(at, 2 * tokens)] = flipped[
-                head * HEAD_DIM : (head + 1) * HEAD_DIM
-            ]
+        for index, block in enumerate(blocks):
+            own = slice(index * size, (index + 1) * size)
+            at = pl.ds(pl.multiple_of((frame * half + block) * size, size), size)
+            for couple in range(heads // 2):
+                keys[couple, at] = projected[own, couple * SLOT : (couple + 1) * SLOT]
+            for head in range(heads):
+                values[head, :HEAD_DIM, at] = flipped[head * HEAD_DIM : (head + 1) * HEAD_DIM, own]
         if with_queries:
-            asked = ((dot(twice, split[0]) + offsets[0, :1]) * scale).astype(BF16)
-            there = pl.ds(pl.multiple_of(block * 2 * tokens, 2 * tokens), 2 * tokens)
-            for head in range(heads):
-                queries[head, there] = asked[:, head * SLOT : (head + 1) * SLOT]
+            asked = ((dot(twice, split_query[...]) + query_offset[:1]) * scale).astype(BF16)
+            for index, block in enumerate(blocks):
+                own = slice(index * size, (index + 1) * size)
+                there = pl.ds(pl.multiple_of(block * size, size), size)
+                for head in range(heads):
+                    queries[head, there] = asked[own, head * SLOT : (head + 1) * SLOT]
 
     def pass_on(step):
         for hop in range(1, half):
             along_ba(step, hop).start()
         to_partner(step, 0).start()
 
-    def frame_step(step, first, with_queries):
+    def advance(step):
+        landed(frame_of(step), ba)
+        pass_on(step)
+
+    def hand_over(step):
         @pl.loop(1, half)
         def _(hop):
             landed(frame_of(step), (ba + n_ba - 2 * hop) % n_ba)
             to_partner(step, hop).start()
 
-        @pl.when(step + 2 < n_aa)
-        def _():
-            landed(frame_of(step + 2), ba)
-            pass_on(step + 2)
-
-        @pl.loop(first, half)
+    def take(step, hop, with_queries):
+        landed(frame_of(step), (partner + n_ba - 2 * hop) % n_ba)
+        take_pairs(step, [hop], with_queries)
+
+    def take_rest(step, with_queries):
+        @pl.loop(1, half)
         def _(hop):
-            landed(frame_of(step), (partner + n_ba - 2 * hop) % n_ba)
-            take_pair(step, hop, with_queries)
+            take(step, hop, with_queries)
 
     for step in range(1, n_aa):
         along_aa(step).start()
     pass_on(0)
     sent(0)
     sent(1)
-    landed(aa, partner)
-    take_pair(0, 0, True)
-    landed(frame_of(1), ba)
-    pass_on(1)
-    frame_step(0, 1, True)
-
-    @pl.loop(1, n_aa)
+    take(0, 0, True)
+    advance(1)
+    hand_over(0)
+
+    @pl.loop(1, half)
+    def _(hop):
+        take(0, hop, True)
+        pl.when(hop + 1 < n_aa)(lambda: advance(hop + 1))
+
+    for step in range(half + 1, n_aa):
+        advance(step)
+    hand_over(1)
+    take(1, 0, False)
+
+    @pl.loop(2, n_aa)
     def _(step):
-        frame_step(step, 0, False)
+        hand_over(step)
+        take_rest(step - 1, False)
+        take(step, 0, False)
+
+    take_rest(n_aa - 1, False)
 
     for step in range(1, n_aa):
         along_aa(step).wait_send()
@@ -411,14 +461,11 @@
             device_id=(aa, dest), device_id_type=MESH,
         )
 
-    per_span = span // tokens
-    spans = n_ba // per_span
     total = keys.shape[1]
     big = math.gcd(total, 4096)
 
-    @pl.loop(0, spans)
-    def _(step):
-        at = (ba // per_span + 1 + step) % spans
+    def attend(at, span, chunk):
+        per_span = span // tokens
         where = pl.ds(pl.multiple_of(at * span, span), span)
 
         def sweep(group, asked, base, state):
@@ -429,7 +476,7 @@
 
             def score(each, part):
                 return lax.dot_general(
-                    keys[group + each, held(part)], asked[each], (((1,), (1,)), ((), ())),
+                    keys[(group + each) // 2, held(part)], asked[each], (((1,), (1,)), ((), ())),
                     preferred_element_type=F32,
                 )
 
@@ -474,10 +521,10 @@
             for each in range(GROUP):
                 accum = state[each][1]
                 rows = pl.ds(pl.multiple_of((group + each) * HEAD_DIM, HEAD_DIM), HEAD_DIM)
-                attended[rows] = (accum[:HEAD_DIM] / accum[HEAD_DIM : HEAD_DIM + 1]).astype(BF16)
+                attended[rows, :span] = (accum[:HEAD_DIM] / accum[HEAD_DIM : HEAD_DIM + 1]).astype(BF16)
 
         velocity = lax.dot_general(
-            w_velocity[...], attended[...], (((0,), (0,)), ((), ())), preferred_element_type=F32
+            w_velocity[...], attended[:, :span], (((0,), (0,)), ((), ())), preferred_element_type=F32
         )
         for part in range(per_span):
             dest = at * per_span + part
@@ -486,6 +533,18 @@
             @pl.when(dest != ba)
             def _():
                 share(dest).start()
+
+    wide = n_ba * tokens // span
+    fine = span // narrow
+    mine = ba * tokens // span
+
+    @pl.loop(1, wide)
+    def _(step):
+        attend((mine + step) % wide, span, chunk)
+
+    @pl.loop(1, fine + 1)
+    def _(step):
+        attend(mine * fine + (ba * tokens // narrow + step) % fine, narrow, 2 * chunk)
 
     summed = shares[ba].astype(F32)
     for offset in range(1, n_ba):
@@ -508,16 +567,26 @@
     tokens = rows * width // 4
     total = n_ba * n_aa * tokens
     span = max(tokens, min(512, n_ba * tokens))
+    narrow = max(tokens, min(256, span))
     chunk = math.gcd(total, 256)
     vmem = pl.BlockSpec(memory_space=pltpu.VMEM)
     anywhere = pl.BlockSpec(memory_space=pl.ANY)
     dma = pltpu.SemaphoreType.DMA
     return pl.pallas_call(
-        functools.partial(whole_kernel, n_aa, n_ba, span, chunk),
+        functools.partial(whole_kernel, n_aa, n_ba, span, narrow, chunk),
         out_shape=jax.ShapeDtypeStruct((tokens, lat), F32),
-        in_specs=[anywhere, anywhere, vmem, anywhere] + [vmem] * 6 + [anywhere] * 3 + [vmem],
+        in_specs=[anywhere] * 14,
         out_specs=vmem,
         scratch_shapes=[
+            pltpu.VMEM((1, chans), F32),
+            pltpu.VMEM((1, chans), F32),
+            pltpu.VMEM((2, 2, chans, lat), BF16),
+            pltpu.VMEM((1, lat), F32),
+            pltpu.VMEM((lat, features), BF16),
+            pltpu.VMEM((1, features), F32),
+            pltpu.VMEM((1, features), F32),
+            pltpu.VMEM((qwidth, lat), BF16),
+            pltpu.VMEM((2 * lat + 16, features), BF16),
             pltpu.VMEM((2, 3, rows + 2, width, chans), BF16),
             pltpu.VMEM((2, 9, chans, 3 * chans), BF16),
             pltpu.VMEM((3, features, qwidth), BF16),
@@ -526,19 +595,21 @@
             pltpu.VMEM((rows, width, chans), F32),
             pltpu.VMEM((2, width, lat), F32),
             pltpu.VMEM((n_aa, n_ba, tokens, lat), BF16),
-            pltpu.VMEM((2, 2 * lat, heads * SLOT), BF16),
-            pltpu.VMEM((2, 8, heads * SLOT), F32),
+            pltpu.VMEM((2 * lat, heads * SLOT), BF16),
+            pltpu.VMEM((8, heads * SLOT), F32),
+            pltpu.VMEM((2 * lat, qwidth), BF16),
+            pltpu.VMEM((8, qwidth), F32),
             pltpu.VMEM((qwidth + 2 * lat, 2 * lat), BF16),
             pltpu.VMEM((qwidth, 8), F32),
             pltpu.VMEM((2 * lat, lat), BF16),
             pltpu.VMEM((lat + 8, lat + 8), F32),
             pltpu.VMEM((heads, n_ba * tokens, SLOT), BF16),
-            pltpu.VMEM((heads, total, SLOT), BF16),
+            pltpu.VMEM((heads // 2, total, SLOT), BF16),
             pltpu.VMEM((heads, STACK, total), BF16),
             pltpu.VMEM((qwidth, span), BF16),
             pltpu.VMEM((n_ba, lat, tokens), BF16),
             pltpu.VMEM((n_ba, lat, tokens), BF16),
-            dma((10,)),
+            dma((10,)), dma((8,)),
             dma((2, 2, 2)), dma((2, 2, 2)), dma((2, 2)), dma((2, 2)),
             dma((n_aa, n_ba)), dma((n_aa,)), dma((n_aa, n_ba // 2)), dma((n_aa, n_ba // 2)),
             dma((n_ba,)), dma((n_ba,)),

time: 64.4 us -> 60.7 us (0.943)
  Pallas kernels: 62.8 us -> 59.1 us
    pallas_call x1, Pallas kernels: 62.8 us -> 59.1 us  [on_device(): pl.pallas_call(functools.partial(whole_kernel, n_aa, n_ba, span, narrow,...]
where the time goes in v2:
time: 60.7 us; the launch traced here: 60.6 us
  Pallas kernels  59.1 us (97%)
  local copies, waits for them, and re-layouts  1.47 us (2%)
    pallas_call x1, Pallas kernels, on_device(): pl.pallas_call(functools.partial(whole_kernel, n_aa, n_ba, span, narrow,...  59.1 us
    unnamed x1, local copies, waits for them, and re-layouts  1.47 us

profile of v2, /device:TPU:0, one launch (start us, length us, event | category | flops | bytes accessed | tf_op | source)
XLA Modules:
  0.0 60.6 jit_solution(10023853401268037572)
XLA Ops:
  0.0 59.1 %whole.1 = f32[128,128]{1,0:T(8,128)} custom-call(bf16[1,4,128,256]{3,2,1,0:T(8,128)(2,1)} %feats.1, bf16[3,9,256,256]{3,2,1,0:T(8,128)(2,1)} %bitcast.7, f32[1,256]{1,0:T(1,128)} %bitcast.11, bf16[3,9,256,256]{3,2,1,0:T(8,128)(2,1)} %bitcast.8, f32[1,256]{1,0:T(1,128)} %bitcast.12, bf16[2,2,256,128]{3,2,1,0:T(8,128)(2,1)} %patch_weight_in.1, ...), custom_call_target="tpu_custom_call" | custom-call | tf_op jit(solution)/shard_map/whole/pallas_call | solution.py:575
  59.1 1.5 %copy.16 = f32[128,128]{1,0:T(8,128)} copy(f32[128,128]{1,0:T(8,128)} %whole.1) | data formatting | bytes 131072

commit v3 on v2

--- a/solution.py
+++ b/solution.py
@@ -11,8 +11,8 @@
 HEAD_DIM = 64
 SLOT = 128
 MESH = pl.DeviceIdType.MESH
-GROUP = 2
-LOOK = 2
+LOOK = 1
+GROUPED = 4
 STACK = HEAD_DIM + 16
 F32 = jnp.float32
 BF16 = jnp.bfloat16
@@ -33,12 +33,12 @@
 
 
 def whole_kernel(
-    n_aa, n_ba, span, narrow, chunk,
+    n_aa, n_ba, span, chunk,
     feats, conv_one, bias_one_in, conv_two, bias_two_in, patch_weight_in, patch_bias_in,
     embed_weight_in, embed_bias_in, norm_gain_in, w_query, w_key, w_value, w_velocity_in,
     out,
     bias_one, bias_two, patch_weight, patch_bias, embed_weight, embed_bias, norm_gain, w_velocity, gained,
-    field, taps, w_joined, outgoing, incoming, acc, pair, gathered, split_query, query_offset, split_key, key_offset, turned, lift,
+    field, taps, w_joined, outgoing, incoming, acc, pair, gathered, turned_query, query_lift, split_key, key_offset, turned, lift,
     gram_split, gram, queries, keys, values, attended, shares, arrived,
     load_sem, small_sem, aa_side_send, aa_side_recv, ba_side_send, ba_side_recv,
     token_recv, aa_send, ba_send, core_send, share_send, share_recv,
@@ -49,6 +49,7 @@
     half = n_ba // 2
     width_q = w_query.shape[1]
     heads = width_q // HEAD_DIM
+    group_size = math.gcd(heads, GROUPED)
     tokens = rows * width // 4
     lat = patch_bias.shape[1]
 
@@ -249,16 +250,10 @@
         product = product[: lat + 8] + product[lat + 8 :]
         if which == 0:
             product = product * (HEAD_DIM**-0.5 * math.log2(math.e))
-            blanks = jnp.zeros((product.shape[0], HEAD_DIM), F32)
-            for head in range(heads):
-                piece = product[:, head * HEAD_DIM : (head + 1) * HEAD_DIM]
-                ordered = (blanks, piece) if head % 2 else (piece, blanks)
-                piece = jnp.concatenate(ordered, axis=1)
-                slot = slice(head * SLOT, (head + 1) * SLOT)
-                high, low = two_parts(piece[:lat])
-                split_query[:lat, slot] = high
-                split_query[lat:, slot] = low
-                query_offset[:, slot] = piece[lat:]
+            high, low = two_parts(product[:lat].T)
+            turned_query[:, :lat] = high
+            turned_query[:, lat:] = low
+            query_lift[...] = product[lat:].T
         elif which == 1:
             high, low = two_parts(product[:lat])
             split_key[:lat] = high
@@ -323,6 +318,9 @@
         ).astype(BF16)
         gathered[aa, ba, pl.ds(block * line, line), :] = patches
 
+    for head in range(heads):
+        slot = slice((1 - head % 2) * HEAD_DIM, (2 - head % 2) * HEAD_DIM)
+        queries[head, slot] = jnp.zeros((HEAD_DIM, queries.shape[2]), BF16)
     values[:, HEAD_DIM:] = jnp.ones((heads, values.shape[1] - HEAD_DIM, values.shape[2]), BF16)
 
     flanked = jnp.minimum(aa, n_aa - 1 - aa)
@@ -383,12 +381,16 @@
             for head in range(heads):
                 values[head, :HEAD_DIM, at] = flipped[head * HEAD_DIM : (head + 1) * HEAD_DIM, own]
         if with_queries:
-            asked = ((dot(twice, split_query[...]) + query_offset[:1]) * scale).astype(BF16)
+            down = lax.dot_general(
+                turned_query[...], twice, (((1,), (1,)), ((), ())), preferred_element_type=F32
+            )
+            asked = ((down + query_lift[:, :1]) * scale_down).astype(BF16)
             for index, block in enumerate(blocks):
                 own = slice(index * size, (index + 1) * size)
                 there = pl.ds(pl.multiple_of(block * size, size), size)
                 for head in range(heads):
-                    queries[head, there] = asked[own, head * SLOT : (head + 1) * SLOT]
+                    slot = slice(head % 2 * HEAD_DIM, (head % 2 + 1) * HEAD_DIM)
+                    queries[head, slot, there] = asked[head * HEAD_DIM : (head + 1) * HEAD_DIM, own]
 
     def pass_on(step):
         for hop in range(1, half):
@@ -464,7 +466,7 @@
     total = keys.shape[1]
     big = math.gcd(total, 4096)
 
-    def attend(at, span, chunk):
+    def attend(at):
         per_span = span // tokens
         where = pl.ds(pl.multiple_of(at * span, span), span)
 
@@ -475,10 +477,7 @@
                 return pl.ds(pl.multiple_of(base + part * chunk, chunk), chunk)
 
             def score(each, part):
-                return lax.dot_general(
-                    keys[(group + each) // 2, held(part)], asked[each], (((1,), (1,)), ((), ())),
-                    preferred_element_type=F32,
-                )
+                return dot(keys[(group + each) // 2, held(part)], asked[each])
 
             def gather(each, part, shrink, probs):
                 best, accum = state[each]
@@ -505,26 +504,26 @@
             state[late[0]] = (state[late[0]][0], gather(*late))
             return state
 
-        @pl.loop(0, heads // GROUP)
+        @pl.loop(0, heads // group_size)
         def _(index):
-            group = index * GROUP
-            asked = [queries[group + each, where] for each in range(GROUP)]
+            group = index * group_size
+            asked = [queries[group + each, :, where] for each in range(group_size)]
             if total == big:
-                state = sweep(group, asked, 0, [(None, None)] * GROUP)
+                state = sweep(group, asked, 0, [(None, None)] * group_size)
             else:
                 empty = (jnp.full((1, span), -jnp.inf, F32), jnp.zeros((values.shape[1], span), F32))
 
                 def one_big(index, state):
                     return tuple(sweep(group, asked, index * big, list(state)))
 
-                state = lax.fori_loop(0, total // big, one_big, (empty,) * GROUP)
-            for each in range(GROUP):
+                state = lax.fori_loop(0, total // big, one_big, (empty,) * group_size)
+            for each in range(group_size):
                 accum = state[each][1]
                 rows = pl.ds(pl.multiple_of((group + each) * HEAD_DIM, HEAD_DIM), HEAD_DIM)
-                attended[rows, :span] = (accum[:HEAD_DIM] / accum[HEAD_DIM : HEAD_DIM + 1]).astype(BF16)
+                attended[rows] = (accum[:HEAD_DIM] / accum[HEAD_DIM : HEAD_DIM + 1]).astype(BF16)
 
         velocity = lax.dot_general(
-            w_velocity[...], attended[:, :span], (((0,), (0,)), ((), ())), preferred_element_type=F32
+            w_velocity[...], attended[...], (((0,), (0,)), ((), ())), preferred_element_type=F32
         )
         for part in range(per_span):
             dest = at * per_span + part
@@ -534,17 +533,11 @@
             def _():
                 share(dest).start()
 
-    wide = n_ba * tokens // span
-    fine = span // narrow
-    mine = ba * tokens // span
-
-    @pl.loop(1, wide)
+    spans = n_ba * tokens // span
+
+    @pl.loop(1, spans + 1)
     def _(step):
-        attend((mine + step) % wide, span, chunk)
-
-    @pl.loop(1, fine + 1)
-    def _(step):
-        attend(mine * fine + (ba * tokens // narrow + step) % fine, narrow, 2 * chunk)
+        attend((ba * tokens // span + step) % spans)
 
     summed = shares[ba].astype(F32)
     for offset in range(1, n_ba):
@@ -567,13 +560,12 @@
     tokens = rows * width // 4
     total = n_ba * n_aa * tokens
     span = max(tokens, min(512, n_ba * tokens))
-    narrow = max(tokens, min(256, span))
     chunk = math.gcd(total, 256)
     vmem = pl.BlockSpec(memory_space=pltpu.VMEM)
     anywhere = pl.BlockSpec(memory_space=pl.ANY)
     dma = pltpu.SemaphoreType.DMA
     return pl.pallas_call(
-        functools.partial(whole_kernel, n_aa, n_ba, span, narrow, chunk),
+        functools.partial(whole_kernel, n_aa, n_ba, span, chunk),
         out_shape=jax.ShapeDtypeStruct((tokens, lat), F32),
         in_specs=[anywhere] * 14,
         out_specs=vmem,
@@ -595,15 +587,15 @@
             pltpu.VMEM((rows, width, chans), F32),
             pltpu.VMEM((2, width, lat), F32),
             pltpu.VMEM((n_aa, n_ba, tokens, lat), BF16),
-            pltpu.VMEM((2 * lat, heads * SLOT), BF16),
-            pltpu.VMEM((8, heads * SLOT), F32),
+            pltpu.VMEM((qwidth, 2 * lat), BF16),
+            pltpu.VMEM((qwidth, 8), F32),
             pltpu.VMEM((2 * lat, qwidth), BF16),
             pltpu.VMEM((8, qwidth), F32),
             pltpu.VMEM((qwidth + 2 * lat, 2 * lat), BF16),
             pltpu.VMEM((qwidth, 8), F32),
             pltpu.VMEM((2 * lat, lat), BF16),
             pltpu.VMEM((lat + 8, lat + 8), F32),
-            pltpu.VMEM((heads, n_ba * tokens, SLOT), BF16),
+            pltpu.VMEM((heads, SLOT, n_ba * tokens), BF16),
             pltpu.VMEM((heads // 2, total, SLOT), BF16),
             pltpu.VMEM((heads, STACK, total), BF16),
             pltpu.VMEM((qwidth, span), BF16),

time: 60.7 us -> 58 us (0.956)
  Pallas kernels: 59.1 us -> 56.3 us
    pallas_call x1, Pallas kernels: 59.1 us -> 56.3 us  [on_device(): pl.pallas_call(functools.partial(whole_kernel, n_aa, n_ba, span, chunk),...]
where the time goes in v3:
time: 58 us; the launch traced here: 57.8 us
  Pallas kernels  56.3 us (97%)
  local copies, waits for them, and re-layouts  1.47 us (3%)
    pallas_call x1, Pallas kernels, on_device(): pl.pallas_call(functools.partial(whole_kernel, n_aa, n_ba, span, chunk),...  56.3 us
    unnamed x1, local copies, waits for them, and re-layouts  1.47 us

profile of v3, /device:TPU:0, one launch (start us, length us, event | category | flops | bytes accessed | tf_op | source)
XLA Modules:
  0.0 57.8 jit_solution(5426052221515057343)
XLA Ops:
  0.0 56.3 %whole.1 = f32[128,128]{1,0:T(8,128)} custom-call(bf16[1,4,128,256]{3,2,1,0:T(8,128)(2,1)} %feats.1, bf16[3,9,256,256]{3,2,1,0:T(8,128)(2,1)} %bitcast.7, f32[1,256]{1,0:T(1,128)} %bitcast.11, bf16[3,9,256,256]{3,2,1,0:T(8,128)(2,1)} %bitcast.8, f32[1,256]{1,0:T(1,128)} %bitcast.12, bf16[2,2,256,128]{3,2,1,0:T(8,128)(2,1)} %patch_weight_in.1, ...), custom_call_target="tpu_custom_call" | custom-call | tf_op jit(solution)/shard_map/whole/pallas_call | solution.py:567
  56.3 1.5 %copy.16 = f32[128,128]{1,0:T(8,128)} copy(f32[128,128]{1,0:T(8,128)} %whole.1) | data formatting | bytes 131072

commit v4 on v3

--- a/solution.py
+++ b/solution.py
@@ -306,17 +306,22 @@
     lines += [inner[at * width : (at + 1) * width] for at in range(rows - 2)]
     lines += [outer[width:]]
 
-    line = width // 2
-    for block in range(rows // 2):
-        for col in range(2):
-            pair[col] = dot(lines[2 * block], patch_weight[0, col]) + dot(
-                lines[2 * block + 1], patch_weight[1, col]
-            )
-        patches = (
-            pair[0, pl.ds(0, line, stride=2), :] + pair[1, pl.ds(1, line, stride=2), :]
-            + patch_bias[...]
-        ).astype(BF16)
-        gathered[aa, ba, pl.ds(block * line, line), :] = patches
+    stacked = jnp.concatenate(
+        [jnp.concatenate(lines[2 * block : 2 * block + 2], axis=1) for block in range(rows // 2)],
+        axis=0,
+    )
+    square = jnp.concatenate(
+        [jnp.concatenate([patch_weight[row, col] for col in range(2)], axis=1) for row in range(2)],
+        axis=0,
+    )
+    both_columns = dot(stacked, square)
+    for col in range(2):
+        pair[col] = both_columns[:, col * lat : (col + 1) * lat]
+    patches = (
+        pair[0, pl.ds(0, tokens, stride=2), :] + pair[1, pl.ds(1, tokens, stride=2), :]
+        + patch_bias[...]
+    ).astype(BF16)
+    gathered[aa, ba] = patches
 
     for head in range(heads):
         slot = slice((1 - head % 2) * HEAD_DIM, (2 - head % 2) * HEAD_DIM)
@@ -411,10 +416,20 @@
         landed(frame_of(step), (partner + n_ba - 2 * hop) % n_ba)
         take_pairs(step, [hop], with_queries)
 
-    def take_rest(step, with_queries):
-        @pl.loop(1, half)
-        def _(hop):
-            take(step, hop, with_queries)
+    def take_all(pairs, with_queries):
+        for step, hop in pairs:
+            landed(frame_of(step), (partner + n_ba - 2 * hop) % n_ba)
+        for step, hop in pairs:
+            take_pairs(step, [hop], with_queries)
+
+    def take_rest(step, also, with_queries):
+        batch = max(each for each in (1, 2, 3) if (half - 1) % each == 0)
+
+        @pl.loop(0, (half - 1) // batch - 1)
+        def _(index):
+            take_all([(step, 1 + index * batch + each) for each in range(batch)], with_queries)
+
+        take_all([(step, half - 1 - each) for each in range(batch)] + also, with_queries)
 
     for step in range(1, n_aa):
         along_aa(step).start()
@@ -438,10 +453,9 @@
     @pl.loop(2, n_aa)
     def _(step):
         hand_over(step)
-        take_rest(step - 1, False)
-        take(step, 0, False)
-
-    take_rest(n_aa - 1, False)
+        take_rest(step - 1, [(step, 0)], False)
+
+    take_rest(n_aa - 1, [], False)
 
     for step in range(1, n_aa):
         along_aa(step).wait_send()
@@ -585,7 +599,7 @@
             pltpu.VMEM((2, 2, rows, width, chans), BF16),
             pltpu.VMEM((2, 2, rows, width, chans), BF16),
             pltpu.VMEM((rows, width, chans), F32),
-            pltpu.VMEM((2, width, lat), F32),
+            pltpu.VMEM((2, rows * width // 2, lat), F32),
             pltpu.VMEM((n_aa, n_ba, tokens, lat), BF16),
             pltpu.VMEM((qwidth, 2 * lat), BF16),
             pltpu.VMEM((qwidth, 8), F32),

time: 58 us -> 56.9 us (0.981)
  Pallas kernels: 56.3 us -> 55.2 us
    pallas_call x1, Pallas kernels: 56.3 us -> 55.2 us  [on_device(): pl.pallas_call(functools.partial(whole_kernel, n_aa, n_ba, span, chunk),...]
where the time goes in v4:
time: 56.9 us; the launch traced here: 56.7 us
  Pallas kernels  55.2 us (97%)
  local copies, waits for them, and re-layouts  1.47 us (3%)
    pallas_call x1, Pallas kernels, on_device(): pl.pallas_call(functools.partial(whole_kernel, n_aa, n_ba, span, chunk),...  55.2 us
    unnamed x1, local copies, waits for them, and re-layouts  1.47 us

profile of v4, /device:TPU:0, one launch (start us, length us, event | category | flops | bytes accessed | tf_op | source)
XLA Modules:
  0.0 56.7 jit_solution(14346868361022013130)
XLA Ops:
  0.0 55.2 %whole.1 = f32[128,128]{1,0:T(8,128)} custom-call(bf16[1,4,128,256]{3,2,1,0:T(8,128)(2,1)} %feats.1, bf16[3,9,256,256]{3,2,1,0:T(8,128)(2,1)} %bitcast.7, f32[1,256]{1,0:T(1,128)} %bitcast.11, bf16[3,9,256,256]{3,2,1,0:T(8,128)(2,1)} %bitcast.8, f32[1,256]{1,0:T(1,128)} %bitcast.12, bf16[2,2,256,128]{3,2,1,0:T(8,128)(2,1)} %patch_weight_in.1, ...), custom_call_target="tpu_custom_call" | custom-call | tf_op jit(solution)/shard_map/whole/pallas_call | solution.py:581
  55.2 1.5 %copy.16 = f32[128,128]{1,0:T(8,128)} copy(f32[128,128]{1,0:T(8,128)} %whole.1) | data formatting | bytes 131072

commit v5 on v4

--- a/solution.py
+++ b/solution.py
@@ -447,13 +447,14 @@
 
     for step in range(half + 1, n_aa):
         advance(step)
+    for step in range(1, n_aa, 3):
+        take_all([(each, 0) for each in range(step, min(step + 3, n_aa))], False)
     hand_over(1)
-    take(1, 0, False)
 
     @pl.loop(2, n_aa)
     def _(step):
         hand_over(step)
-        take_rest(step - 1, [(step, 0)], False)
+        take_rest(step - 1, [], False)
 
     take_rest(n_aa - 1, [], False)
 

time: 56.9 us -> 56.5 us (level)
  no operation moved by 1% of the time
where the time goes in v5:
time: 56.5 us; the launch traced here: 56.4 us
  Pallas kernels  54.9 us (97%)
  local copies, waits for them, and re-layouts  1.47 us (3%)
    pallas_call x1, Pallas kernels, on_device(): pl.pallas_call(functools.partial(whole_kernel, n_aa, n_ba, span, chunk),...  54.9 us
    unnamed x1, local copies, waits for them, and re-layouts  1.47 us

profile of v5, /device:TPU:0, one launch (start us, length us, event | category | flops | bytes accessed | tf_op | source)
XLA Modules:
  0.0 56.4 jit_solution(8447413127157220200)
XLA Ops:
  0.0 54.9 %whole.1 = f32[128,128]{1,0:T(8,128)} custom-call(bf16[1,4,128,256]{3,2,1,0:T(8,128)(2,1)} %feats.1, bf16[3,9,256,256]{3,2,1,0:T(8,128)(2,1)} %bitcast.7, f32[1,256]{1,0:T(1,128)} %bitcast.11, bf16[3,9,256,256]{3,2,1,0:T(8,128)(2,1)} %bitcast.8, f32[1,256]{1,0:T(1,128)} %bitcast.12, bf16[2,2,256,128]{3,2,1,0:T(8,128)(2,1)} %patch_weight_in.1, ...), custom_call_target="tpu_custom_call" | custom-call | tf_op jit(solution)/shard_map/whole/pallas_call | solution.py:582
  54.9 1.5 %copy.16 = f32[128,128]{1,0:T(8,128)} copy(f32[128,128]{1,0:T(8,128)} %whole.1) | data formatting | bytes 131072
